TPU v7x, 32 devices: a whole 2x2x4 slice. The times are simulated.
32 devices in a mesh: parts: 2 (over y), tm: 16 (over z, x, core).
Axes of the slice: x: 2, y: 2, z: 4, core: 2. Of those that a mesh axis runs over, the one named last changes fastest.
Arguments:
- frames: bfloat16 [2048, 2048], P('tm', 'parts'), parts along dimension 1, may hold values from -6 to 6
- levels: int32 [2048], P(('parts', 'tm')), parts along dimension 0, may hold values from 0 to 15
- initial_state: float32 [256], P('parts'), parts along dimension 0, may hold values from -6 to 6
- transitions: float32 [16, 128, 128], replicated, may hold values from -1 to 1
- gain: bfloat16 [128, 128], replicated, may hold values from -1 to 1
- pixel_mode: int32 [2048], replicated, may hold values from 0 to 127
- pixel_weight: bfloat16 [2048], replicated, may hold values from 0.099609375 to 0.5
Outputs:
- estimates: float32 [2048, 128], P(('parts', 'tm')), parts along dimension 0
There are 2 independent parts, one for each index of `parts`. A program takes and returns all parts, laid end to end along the dimension named above; an argument that names none is the same for every part. Nothing has to cross between parts.
All inputs are finite; a program needn't handle non-finite values.
Results may differ from a plain program's by a relative error of at most 0.0026.
Values may be sent and summed in bfloat16 or wider, within the bound.
A program may use at most 128 MiB of HBM per device.

v0:
```python
import functools

import jax
import jax.numpy as jnp
from jax import lax
from jax.experimental import pallas as pl
from jax.experimental.pallas import tpu as pltpu
from jax.sharding import PartitionSpec as P

MESH = pl.DeviceIdType.MESH
F32 = jnp.float32
BF16 = jnp.bfloat16
STEPS = 8


def halves(x):
    high = x.astype(BF16)
    return high, (x - high.astype(F32)).astype(BF16)


def left_pair(x):
    high, low = halves(x)
    return jnp.concatenate([high, low], axis=1)


def right_pair(y):
    pair = left_pair(y)
    return jnp.concatenate([pair, pair], axis=0)


def joined(pair):
    return pair[:, : pair.shape[1] // 2] + pair[:, pair.shape[1] // 2 :]


def product(x, y):
    return joined(jnp.dot(left_pair(x), right_pair(y), preferred_element_type=F32))


def diagonal(size):
    return lax.broadcasted_iota(jnp.int32, (size, size), 0) == lax.broadcasted_iota(
        jnp.int32, (size, size), 1
    )


def to_column(eye, row):
    return jnp.sum(jnp.where(eye, row, 0.0), axis=1, keepdims=True)


def to_row(eye, column):
    return jnp.sum(jnp.where(eye, column, 0.0), axis=0, keepdims=True)


def row_step(eye, matrix, row, push):
    return jnp.sum(matrix * row + jnp.where(eye, push, 0.0), axis=1, keepdims=True)


def column_step(flipped, column, push):
    return jnp.sum(flipped * column, axis=0, keepdims=True) + push


def maps_kernel(levels, table, flipped, prefix, heads, ends, total, pairs):
    count = levels.shape[0] // STEPS
    for level in range(table.shape[0]):
        turned = table[level].T
        flipped[level] = turned
        pairs[level] = right_pair(turned)
    for chunk in range(count):
        prefix[chunk * STEPS] = flipped[levels[chunk * STEPS]]
    for step in range(1, STEPS):
        for chunk in range(count):
            t = chunk * STEPS + step
            prefix[t] = joined(
                jnp.dot(left_pair(prefix[t - 1]), pairs[levels[t]], preferred_element_type=F32)
            )
    spans = [prefix[chunk * STEPS + STEPS - 1] for chunk in range(count)]
    for chunk in range(count):
        ends[chunk] = spans[chunk].T if chunk % 2 else spans[chunk]
    width = 1
    while width < count:
        for chunk in range(count):
            if chunk & width:
                base = (chunk // width) * width - 1
                spans[chunk] = product(spans[base], spans[chunk])
        width *= 2
    for chunk in range(count - 1):
        heads[chunk] = spans[chunk].T
    total[0] = spans[count - 1]
    total[1] = spans[count - 1].T


def exchange_kernel(n, group, frames, total, regrouped, maps, own_sem, send_sem, recv_sem, msend_sem, mrecv_sem):
    me = lax.axis_index("tm")
    span = regrouped.shape[1]
    barrier = pltpu.get_barrier_semaphore()

    @pl.loop(1, n)
    def _(away):
        pl.semaphore_signal(barrier, inc=1, device_id={"tm": lax.rem(me + away, n)}, device_id_type=MESH)

    home = (me // group) * group
    place = lax.rem(me, group)
    own = pltpu.make_async_copy(
        frames.at[pl.ds(pl.multiple_of(me * span, span), span)], regrouped.at[me], own_sem.at[0]
    )
    own.start()
    kept = pltpu.make_async_copy(total.at[lax.rem(place, 2)], maps.at[place], own_sem.at[1])
    kept.start()
    pl.semaphore_wait(barrier, n - 1)

    def piece(away):
        target = lax.rem(me + away, n)
        return pltpu.make_async_remote_copy(
            src_ref=frames.at[pl.ds(pl.multiple_of(target * span, span), span)],
            dst_ref=regrouped.at[me],
            send_sem=send_sem.at[away],
            recv_sem=recv_sem.at[away],
            device_id={"tm": target},
            device_id_type=MESH,
        )

    def shared(away):
        return pltpu.make_async_remote_copy(
            src_ref=total.at[lax.rem(place, 2)],
            dst_ref=maps.at[place],
            send_sem=msend_sem.at[away],
            recv_sem=mrecv_sem.at[away],
            device_id={"tm": home + lax.rem(place + away, group)},
            device_id_type=MESH,
        )

    @pl.loop(1, n)
    def _(away):
        piece(away).start()

    @pl.loop(1, group)
    def _(away):
        shared(away).start()

    own.wait()
    kept.wait()

    @pl.loop(1, n)
    def _(away):
        piece(away).wait()

    @pl.loop(1, group)
    def _(away):
        shared(away).wait()


def local_kernel(levels, regrouped, modes, weights, gain, table, flipped, ends, maps, local, chunk_ends, whole):
    n, frames, pixels = regrouped.shape
    states = gain.shape[0]
    eye = diagonal(states)
    channels = lax.broadcasted_iota(jnp.int32, (states, pixels), 0)
    measured = jnp.zeros((frames, states), F32)
    for k in range(n):
        projector = jnp.where(modes[k : k + 1] == channels, weights[k : k + 1].astype(F32), 0.0)
        measured += lax.dot_general(
            regrouped[k], projector.astype(BF16), (((1,), (1,)), ((), ())), preferred_element_type=F32
        )
    local[...] = lax.dot_general(
        measured.astype(BF16), gain[...], (((1,), (1,)), ((), ())), preferred_element_type=F32
    )
    count = frames // STEPS
    held = [to_column(eye, local[c * STEPS : c * STEPS + 1]) for c in range(count)]
    for step in range(1, STEPS):
        for c in range(count):
            t = c * STEPS + step
            push = local[t : t + 1]
            if step % 2:
                held[c] = column_step(flipped[levels[t]], held[c], push)
                local[t : t + 1] = held[c]
            else:
                held[c] = row_step(eye, table[levels[t]], held[c], push)
                local[t : t + 1] = to_row(eye, held[c])
    carried = local[STEPS - 1 : STEPS]
    chunk_ends[0:1] = carried
    for c in range(1, count):
        push = local[c * STEPS + STEPS - 1 : c * STEPS + STEPS]
        if c % 2:
            carried = row_step(eye, ends[c], carried, push)
            chunk_ends[c : c + 1] = to_row(eye, carried)
        else:
            carried = column_step(ends[c], carried, push)
            chunk_ends[c : c + 1] = carried
    group = maps.shape[0]
    chain = maps[0].T
    for k in range(1, group):
        chain = product(maps[k] if k % 2 else maps[k].T, chain)
    whole[...] = chain


def chain_kernel(n, group, shift, maps, whole, start, incoming, shifts, arrived, leaving, send_sem, recv_sem, hop_send, hop_recv):
    me = lax.axis_index("tm")
    place = lax.rem(me, group)
    home = me - place
    states = whole.shape[0]
    eye = diagonal(states)
    has_next = me + group < n
    has_last = me >= group
    barrier = pltpu.get_barrier_semaphore()
    for away in range(1, group):
        pl.semaphore_signal(
            barrier, inc=1, device_id={"tm": home + lax.rem(place + away, group)}, device_id_type=MESH
        )

    @pl.when(has_last)
    def _():
        pl.semaphore_signal(barrier, inc=1, device_id={"tm": me - group}, device_id_type=MESH)

    shifts[place] = shift[...]
    pl.semaphore_wait(barrier, jnp.where(has_next, group, group - 1))

    def shared(away):
        return pltpu.make_async_remote_copy(
            src_ref=shift,
            dst_ref=shifts.at[place],
            send_sem=send_sem.at[away],
            recv_sem=recv_sem.at[away],
            device_id={"tm": home + lax.rem(place + away, group)},
            device_id_type=MESH,
        )

    for away in range(1, group):
        shared(away).start()
    for away in range(1, group):
        shared(away).wait()
    moved = shifts[0, 0:1]
    for k in range(1, group):
        push = shifts[k, 0:1]
        moved = row_step(eye, maps[k], moved, push) if k % 2 else column_step(maps[k], moved, push)
    offset = moved if group % 2 else to_row(eye, moved)

    hop = pltpu.make_async_remote_copy(
        src_ref=leaving,
        dst_ref=arrived,
        send_sem=hop_send.at[0],
        recv_sem=hop_recv.at[0],
        device_id={"tm": lax.rem(me + group, n)},
        device_id_type=MESH,
    )

    @pl.when(has_last)
    def _():
        hop.wait_recv()

    @pl.when(jnp.logical_not(has_last))
    def _():
        arrived[...] = jnp.broadcast_to(start[...], arrived.shape)

    entry = arrived[0:1]

    @pl.when(has_next)
    def _():
        leaving[...] = jnp.broadcast_to(
            to_row(eye, row_step(eye, whole[...], entry, offset)), leaving.shape
        )
        hop.start()

    inside = entry
    column = to_column(eye, entry)
    for k in range(group - 1):
        push = shifts[k, 0:1]
        if k % 2:
            column = row_step(eye, maps[k], row, push)
            after = to_row(eye, column)
        else:
            row = column_step(maps[k], column, push)
            after = row
        inside = jnp.where(place == k + 1, after, inside)
    incoming[...] = inside

    @pl.when(has_next)
    def _():
        hop.wait_send()


def finish_kernel(incoming, heads, chunk_ends, prefix, local, out):
    frames, states = local.shape
    eye = diagonal(states)
    entry = incoming[...]
    for c in range(frames // STEPS):
        if c:
            column = row_step(eye, heads[c - 1], entry, chunk_ends[c - 1 : c])
        else:
            column = to_column(eye, entry)
        for step in range(STEPS):
            t = c * STEPS + step
            out[t : t + 1] = column_step(prefix[t], column, local[t : t + 1])


VMEM = pl.BlockSpec(memory_space=pltpu.VMEM)
SMEM = pl.BlockSpec(memory_space=pltpu.SMEM)
ANY = pl.BlockSpec(memory_space=pl.ANY)
LIMIT = 48 * 1024 * 1024


def shape(*dims, dtype=F32):
    return jax.ShapeDtypeStruct(dims, dtype)


def shards(n, frames, levels, initial_state, transitions, gain, pixel_mode, pixel_weight):
    group = 4
    while n % group:
        group //= 2
    span = levels.shape[0]
    depth, states = transitions.shape[0], transitions.shape[1]
    pixels = frames.shape[0]
    count = span // STEPS
    plain = pltpu.CompilerParams(vmem_limit_bytes=LIMIT)
    flipped, prefix, heads, ends, total = pl.pallas_call(
        maps_kernel,
        out_shape=(
            shape(depth, states, states),
            shape(span, states, states),
            shape(count - 1, states, states),
            shape(count, states, states),
            shape(2, states, states),
        ),
        in_specs=[SMEM, VMEM],
        out_specs=(VMEM,) * 5,
        scratch_shapes=[pltpu.VMEM((depth, 2 * states, 2 * states), BF16)],
        compiler_params=plain,
        name="maps",
    )(levels, transitions)
    regrouped, maps = pl.pallas_call(
        functools.partial(exchange_kernel, n, group),
        out_shape=(shape(n, span, pixels, dtype=BF16), shape(group, states, states)),
        in_specs=[ANY, ANY],
        out_specs=(ANY, ANY),
        scratch_shapes=[
            pltpu.SemaphoreType.DMA((2,)),
            pltpu.SemaphoreType.DMA((n,)),
            pltpu.SemaphoreType.DMA((n,)),
            pltpu.SemaphoreType.DMA((group,)),
            pltpu.SemaphoreType.DMA((group,)),
        ],
        compiler_params=pltpu.CompilerParams(collective_id=0, has_side_effects=True),
        name="exchange",
    )(frames.T, total)
    local, chunk_ends, whole = pl.pallas_call(
        local_kernel,
        out_shape=(shape(span, states), shape(count, states), shape(states, states)),
        in_specs=[SMEM] + [VMEM] * 8,
        out_specs=(VMEM,) * 3,
        compiler_params=plain,
        name="local",
    )(
        levels,
        regrouped,
        pixel_mode.reshape(n, pixels),
        pixel_weight.reshape(n, pixels),
        gain,
        transitions,
        flipped,
        ends,
        maps,
    )
    shift = jnp.broadcast_to(chunk_ends[count - 1 :], (8, states))
    incoming = pl.pallas_call(
        functools.partial(chain_kernel, n, group),
        out_shape=shape(1, states),
        in_specs=[VMEM] * 4,
        out_specs=VMEM,
        scratch_shapes=[
            pltpu.VMEM((group, 8, states), F32),
            pltpu.VMEM((8, states), F32),
            pltpu.VMEM((8, states), F32),
            pltpu.SemaphoreType.DMA((group,)),
            pltpu.SemaphoreType.DMA((group,)),
            pltpu.SemaphoreType.DMA((1,)),
            pltpu.SemaphoreType.DMA((1,)),
        ],
        compiler_params=pltpu.CompilerParams(collective_id=1, has_side_effects=True),
        name="chain",
    )(shift, maps, whole, initial_state.reshape(1, states))
    return pl.pallas_call(
        finish_kernel,
        out_shape=shape(span, states),
        in_specs=[VMEM] * 5,
        out_specs=VMEM,
        compiler_params=plain,
        name="finish",
    )(incoming, heads, chunk_ends, prefix, local)


def solution(mesh):
    in_specs = (P("tm", "parts"), P(("parts", "tm")), P("parts"), P(), P(), P(), P())
    out_specs = P(("parts", "tm"), None)
    return jax.shard_map(
        functools.partial(shards, mesh.shape["tm"]),
        mesh=mesh,
        in_specs=in_specs,
        out_specs=out_specs,
        check_vma=False,
    )
```

profile of v0, /device:TPU:24, one launch (start us, length us, event | category | flops | bytes accessed | tf_op | source)
XLA Modules:
  0.0 45.8 jit_solution(17648757001516627791)
XLA Ops:
  0.0 1.8 %copy.8 = bf16[128,1024]{0,1:T(8,128)(2,1)} copy(bf16[128,1024]{1,0:T(8,128)(2,1)} %param.7) | data formatting | bytes 524288 | tf_op args[0]
  1.8 0.0 copy-start.1
  1.8 1.2 %copy-done.1 = f32[16,128,128]{2,1,0:T(8,128)S(1)} copy-done((f32[16,128,128]{2,1,0:T(8,128)S(1)}, f32[16,128,128]{2,1,0:T(8,128)}, u32[]{:S(2)}) %copy-start.1) | copy-done | bytes 1048600
  3.0 0.0 copy-start.11
  3.0 0.7 %copy-done.11 = s32[64]{0:T(128)S(1)} copy-done((s32[64]{0:T(128)S(1)}, s32[64]{0:T(128)}, u32[]{:S(2)}) %copy-start.11) | copy-done | bytes 280
  3.7 4.0 %maps.1 = (f32[16,128,128]{2,1,0:T(8,128)S(1)}, f32[64,128,128]{2,1,0:T(8,128)}, f32[7,128,128]{2,1,0:T(8,128)S(1)}, f32[8,128,128]{2,1,0:T(8,128)S(1)}, f32[2,128,128]{2,1,0:T(8,128)S(1)}) custom-call(s32[64]{0:T(128)S(1)} %copy-done.11, f32[16,128,128]{2,1,0:T(8,128)S(1)} %copy-done.1), custom_call_target="tpu_custom_call" | custom-call | tf_op jit(solution)/shard_map/maps/pallas_call | solution.py:312
  7.7 0.0 copy-start.5
  7.7 0.6 %copy-done.5 = f32[2,128,128]{2,1,0:T(8,128)} copy-done((f32[2,128,128]{2,1,0:T(8,128)}, f32[2,128,128]{2,1,0:T(8,128)S(1)}, u32[]{:S(2)}) %copy-start.5) | copy-done | bytes 131096
  8.3 10.2 %exchange.1 = (bf16[16,64,128]{2,1,0:T(8,128)(2,1)}, f32[4,128,128]{2,1,0:T(8,128)}) custom-call(bf16[1024,128]{1,0:T(8,128)(2,1)} %bitcast.8, f32[2,128,128]{2,1,0:T(8,128)} %copy-done.5), custom_call_target="tpu_custom_call" | custom-call | tf_op jit(solution)/shard_map/exchange/pallas_call | solution.py:327
  18.5 0.0 copy-start.2
  18.5 1.2 %copy-done.2 = f32[16,128,128]{2,1,0:T(8,128)S(1)} copy-done((f32[16,128,128]{2,1,0:T(8,128)S(1)}, f32[16,128,128]{2,1,0:T(8,128)}, u32[]{:S(2)}) %copy-start.2) | copy-done | bytes 1048600
  19.8 0.0 copy-start.3
  19.8 0.9 %copy-done.3 = f32[4,128,128]{2,1,0:T(8,128)S(1)} copy-done((f32[4,128,128]{2,1,0:T(8,128)S(1)}, f32[4,128,128]{2,1,0:T(8,128)}, u32[]{:S(2)}) %copy-start.3) | copy-done | bytes 262168
  20.7 0.0 copy-start.4
  20.7 0.9 %copy-done.4 = bf16[16,64,128]{2,1,0:T(8,128)(2,1)S(1)} copy-done((bf16[16,64,128]{2,1,0:T(8,128)(2,1)S(1)}, bf16[16,64,128]{2,1,0:T(8,128)(2,1)}, u32[]{:S(2)}) %copy-start.4) | copy-done | bytes 262168
  21.7 0.0 copy-start.7
  21.7 0.8 %copy-done.7 = bf16[128,128]{1,0:T(8,128)(2,1)S(1)} copy-done((bf16[128,128]{1,0:T(8,128)(2,1)S(1)}, bf16[128,128]{1,0:T(8,128)(2,1)}, u32[]{:S(2)}) %copy-start.7) | copy-done | bytes 32792
  22.4 0.0 copy-start.8
  22.4 0.7 %copy-done.8 = s32[2048]{0:T(1024)S(1)} copy-done((s32[2048]{0:T(1024)S(1)}, s32[2048]{0:T(1024)}, u32[]{:S(2)}) %copy-start.8) | copy-done | bytes 8216
  23.1 0.0 copy-start.9
  23.1 0.7 %copy-done.9 = bf16[2048]{0:T(1024)(128)(2,1)S(1)} copy-done((bf16[2048]{0:T(1024)(128)(2,1)S(1)}, bf16[2048]{0:T(1024)(128)(2,1)}, u32[]{:S(2)}) %copy-start.9) | copy-done | bytes 4120
  23.8 0.0 copy-start.12
  23.8 0.7 %copy-done.12 = s32[64]{0:T(128)S(1)} copy-done((s32[64]{0:T(128)S(1)}, s32[64]{0:T(128)}, u32[]{:S(2)}) %copy-start.12) | copy-done | bytes 280
  24.5 2.2 %local.1 = (f32[64,128]{1,0:T(8,128)S(1)}, f32[8,128]{1,0:T(8,128)S(1)}, f32[128,128]{1,0:T(8,128)S(1)}) custom-call(s32[64]{0:T(128)S(1)} %copy-done.12, bf16[16,64,128]{2,1,0:T(8,128)(2,1)S(1)} %copy-done.4, s32[16,128]{1,0:T(8,128)S(1)} %bitcast.6, bf16[16,128]{1,0:T(8,128)(2,1)S(1)} %bitcast.7, bf16[128,128]{1,0:T(8,128)(2,1)S(1)} %copy-done.7, ...), custom_call_target="tpu_custom_call" | custom-call | tf_op jit(solution)/shard_map/local/pallas_call | solution.py:342
  26.7 0.0 copy-start.6
  26.7 0.6 %copy-done.6 = f32[128,128]{1,0:T(8,128)} copy-done((f32[128,128]{1,0:T(8,128)}, f32[128,128]{1,0:T(8,128)S(1)}, u32[]{:S(2)}) %copy-start.6) | copy-done | bytes 65560
  27.3 0.6 %broadcast_in_dim.8.shift = f32[8,128]{1,0:T(8,128)} broadcast(f32[128]{0:T(128)S(1)} %slice_bitcast_fusion), dimensions={1} | broadcast | bytes 4608 | tf_op jit(solution)/shard_map/broadcast_in_dim | solution.py:360
  27.9 13.9 %chain.1.incoming = f32[1,128]{1,0:T(1,128)} custom-call(f32[8,128]{1,0:T(8,128)} %broadcast_in_dim.8.shift, f32[4,128,128]{2,1,0:T(8,128)} %get-tuple-element.19.maps, f32[128,128]{1,0:T(8,128)} %copy-done.6, f32[1,128]{1,0:T(1,128)} %bitcast.9), custom_call_target="tpu_custom_call" | custom-call | tf_op jit(solution)/shard_map/chain/pallas_call | solution.py:361
  41.9 0.0 copy-start
  41.9 2.2 %copy-done = f32[64,128,128]{2,1,0:T(8,128)S(1)} copy-done((f32[64,128,128]{2,1,0:T(8,128)S(1)}, f32[64,128,128]{2,1,0:T(8,128)}, u32[]{:S(2)}) %copy-start) | copy-done | bytes 4194328
  44.1 0.7 %copy-done.10 = f32[1,128]{1,0:T(1,128)S(1)} copy-done((f32[1,128]{1,0:T(1,128)S(1)}, f32[1,128]{1,0:T(1,128)}, u32[]{:S(2)}) %copy-start.10) | copy-done | bytes 536
  44.7 1.1 %finish.1 = f32[64,128]{1,0:T(8,128)} custom-call(f32[1,128]{1,0:T(1,128)S(1)} %copy-done.10, f32[7,128,128]{2,1,0:T(8,128)S(1)} %get-tuple-element.22.heads, f32[8,128]{1,0:T(8,128)S(1)} %get-tuple-element.20.chunk_ends, f32[64,128,128]{2,1,0:T(8,128)S(1)} %copy-done, f32[64,128]{1,0:T(8,128)S(1)} %get-tuple-element.24.local), custom_call_target="tpu_custom_call" | custom-call | tf_op jit(solution)/shard_map/finish/pallas_call | solution.py:378
  (2 shorter events, 0.0 us)
Async XLA Ops:
  1.8 1.2 %copy-start.1 = (f32[16,128,128]{2,1,0:T(8,128)S(1)}, f32[16,128,128]{2,1,0:T(8,128)}, u32[]{:S(2)}) copy-start(f32[16,128,128]{2,1,0:T(8,128)} %table.3) | copy-start | bytes 3145732
  3.0 0.7 %copy-start.11 = (s32[64]{0:T(128)S(1)}, s32[64]{0:T(128)}, u32[]{:S(2)}) copy-start(s32[64]{0:T(128)} %levels.3) | copy-start | bytes 772
  7.7 0.6 %copy-start.5 = (f32[2,128,128]{2,1,0:T(8,128)}, f32[2,128,128]{2,1,0:T(8,128)S(1)}, u32[]{:S(2)}) copy-start(f32[2,128,128]{2,1,0:T(8,128)S(1)} %get-tuple-element.15.total) | copy-start | bytes 393220
  18.5 1.2 %copy-start.2 = (f32[16,128,128]{2,1,0:T(8,128)S(1)}, f32[16,128,128]{2,1,0:T(8,128)}, u32[]{:S(2)}) copy-start(f32[16,128,128]{2,1,0:T(8,128)} %table.3) | copy-start | bytes 3145732
  19.8 0.9 %copy-start.3 = (f32[4,128,128]{2,1,0:T(8,128)S(1)}, f32[4,128,128]{2,1,0:T(8,128)}, u32[]{:S(2)}) copy-start(f32[4,128,128]{2,1,0:T(8,128)} %get-tuple-element.19.maps) | copy-start | bytes 786436
  20.7 0.9 %copy-start.4 = (bf16[16,64,128]{2,1,0:T(8,128)(2,1)S(1)}, bf16[16,64,128]{2,1,0:T(8,128)(2,1)}, u32[]{:S(2)}) copy-start(bf16[16,64,128]{2,1,0:T(8,128)(2,1)} %get-tuple-element.16.regrouped) | copy-start | bytes 786436
  21.7 0.8 %copy-start.7 = (bf16[128,128]{1,0:T(8,128)(2,1)S(1)}, bf16[128,128]{1,0:T(8,128)(2,1)}, u32[]{:S(2)}) copy-start(bf16[128,128]{1,0:T(8,128)(2,1)} %gain.1) | copy-start | bytes 98308
  22.4 0.7 %copy-start.8 = (s32[2048]{0:T(1024)S(1)}, s32[2048]{0:T(1024)}, u32[]{:S(2)}) copy-start(s32[2048]{0:T(1024)} %param.12) | copy-start | bytes 24580
  23.1 0.7 %copy-start.9 = (bf16[2048]{0:T(1024)(128)(2,1)S(1)}, bf16[2048]{0:T(1024)(128)(2,1)}, u32[]{:S(2)}) copy-start(bf16[2048]{0:T(1024)(128)(2,1)} %param.13) | copy-start | bytes 12292
  23.8 0.7 %copy-start.12 = (s32[64]{0:T(128)S(1)}, s32[64]{0:T(128)}, u32[]{:S(2)}) copy-start(s32[64]{0:T(128)} %levels.3) | copy-start | bytes 772
  26.7 0.6 %copy-start.6 = (f32[128,128]{1,0:T(8,128)}, f32[128,128]{1,0:T(8,128)S(1)}, u32[]{:S(2)}) copy-start(f32[128,128]{1,0:T(8,128)S(1)} %get-tuple-element.21.whole) | copy-start | bytes 196612
  41.9 2.2 %copy-start = (f32[64,128,128]{2,1,0:T(8,128)S(1)}, f32[64,128,128]{2,1,0:T(8,128)}, u32[]{:S(2)}) copy-start(f32[64,128,128]{2,1,0:T(8,128)} %get-tuple-element.23.prefix) | copy-start | bytes 12582916
  44.1 0.7 %copy-start.10 = (f32[1,128]{1,0:T(1,128)S(1)}, f32[1,128]{1,0:T(1,128)}, u32[]{:S(2)}) copy-start(f32[1,128]{1,0:T(1,128)} %chain.1.incoming) | copy-start | bytes 1540
where the time goes:
time: 46.3 us; the launch traced here: 45.8 us
  Pallas kernels  31.4 us (68%)
  local copies, waits for them, and re-layouts  14.3 us (31%)
    pallas_call x1, Pallas kernels, shards(): pl.pallas_call(functools.partial(chain_kernel, n, group), out_shape=shape...  13.9 us
    unnamed x27, local copies, waits for them, and re-layouts  13.7 us
    pallas_call x1, Pallas kernels, shards(): pl.pallas_call(functools.partial(exchange_kernel, n, group), out_shape=(s...  10.2 us
    pallas_call x1, Pallas kernels, shards(): pl.pallas_call(maps_kernel, out_shape=(shape(depth, states, states), shap...  4.01 us
    pallas_call x1, Pallas kernels, shards(): pl.pallas_call(local_kernel, out_shape=(shape(span, states), shape(count,...  2.23 us
    pallas_call x1, Pallas kernels, shards(): pl.pallas_call(finish_kernel, out_shape=shape(span, states), in_specs=[VM...  1.06 us

commit v1 on v0

v1 whole, which is shorter than its diff:
```python
import functools

import jax
import jax.numpy as jnp
from jax import lax
from jax.experimental import pallas as pl
from jax.experimental.pallas import tpu as pltpu
from jax.sharding import PartitionSpec as P

MESH = pl.DeviceIdType.MESH
F32 = jnp.float32
BF16 = jnp.bfloat16
STEPS = 8


def halves(x):
    high = x.astype(BF16)
    return high, (x - high.astype(F32)).astype(BF16)


def left_pair(x):
    high, low = halves(x)
    return jnp.concatenate([high, low], axis=1)


def right_pair(y):
    pair = left_pair(y)
    return jnp.concatenate([pair, pair], axis=0)


def joined(pair):
    return pair[:, : pair.shape[1] // 2] + pair[:, pair.shape[1] // 2 :]


def product(x, y):
    return joined(jnp.dot(left_pair(x), right_pair(y), preferred_element_type=F32))


def diagonal(size):
    return lax.broadcasted_iota(jnp.int32, (size, size), 0) == lax.broadcasted_iota(
        jnp.int32, (size, size), 1
    )


def to_column(eye, row):
    return jnp.sum(jnp.where(eye, row, 0.0), axis=1, keepdims=True)


def to_row(eye, column):
    return jnp.sum(jnp.where(eye, column, 0.0), axis=0, keepdims=True)


def row_step(eye, matrix, row, push):
    return jnp.sum(matrix * row + jnp.where(eye, push, 0.0), axis=1, keepdims=True)


def column_step(flipped, column, push):
    return jnp.sum(flipped * column, axis=0, keepdims=True) + push


def fused_kernel(
    n, group,
    levels, frames_in, table_in, gain_in, modes_in, weights_in, start_in,
    out,
    raw, turned, regrouped, table, flipped, pairs, prefix, heads, ends, total, maps, whole,
    gain, modes, weights, start, projector, local, chunk_ends, shift, shifts, arrived, leaving,
    load_sem, own_sem, send_sem, recv_sem, msend_sem, mrecv_sem, csend_sem, crecv_sem, hop_send, hop_recv,
):
    me = lax.axis_index("tm")
    place = lax.rem(me, group)
    home = me - place
    has_next = me + group < n
    has_last = me >= group
    span = out.shape[0]
    states = gain.shape[0]
    pixels = raw.shape[0]
    count = span // STEPS
    loads = [
        pltpu.make_async_copy(source, target, load_sem.at[i])
        for i, (source, target) in enumerate(
            [(frames_in, raw), (table_in, table), (gain_in, gain), (modes_in, modes), (weights_in, weights), (start_in, start)]
        )
    ]
    for load in loads:
        load.start()
    barrier = pltpu.get_barrier_semaphore()

    @pl.loop(1, n)
    def _(away):
        pl.semaphore_signal(barrier, inc=1, device_id={"tm": lax.rem(me + away, n)}, device_id_type=MESH)

    loads[0].wait()
    for block in range(0, n * span, 128):
        turned[block : block + 128] = raw[:, block : block + 128].T
    pl.semaphore_wait(barrier, n - 1)

    def piece(away):
        target = lax.rem(me + away, n)
        return pltpu.make_async_remote_copy(
            src_ref=turned.at[pl.ds(pl.multiple_of(target * span, span), span)],
            dst_ref=regrouped.at[me],
            send_sem=send_sem.at[away],
            recv_sem=recv_sem.at[away],
            device_id={"tm": target},
            device_id_type=MESH,
        )

    @pl.loop(1, n)
    def _(away):
        piece(away).start()

    own = pltpu.make_async_copy(
        turned.at[pl.ds(pl.multiple_of(me * span, span), span)], regrouped.at[me], own_sem.at[0]
    )
    own.start()

    loads[1].wait()
    for level in range(table.shape[0]):
        other = table[level].T
        flipped[level] = other
        pairs[level] = right_pair(other)
    for chunk in range(count):
        prefix[chunk * STEPS] = flipped[levels[chunk * STEPS]]
    for step in range(1, STEPS):
        for chunk in range(count):
            t = chunk * STEPS + step
            prefix[t] = joined(
                jnp.dot(left_pair(prefix[t - 1]), pairs[levels[t]], preferred_element_type=F32)
            )
    spans = [prefix[chunk * STEPS + STEPS - 1] for chunk in range(count)]
    for chunk in range(count):
        ends[chunk] = spans[chunk].T if chunk % 2 else spans[chunk]
    width = 1
    while width < count:
        for chunk in range(count):
            if chunk & width:
                base = (chunk // width) * width - 1
                spans[chunk] = product(spans[base], spans[chunk])
        width *= 2
    total[0] = spans[count - 1]
    total[1] = spans[count - 1].T

    def shared(away):
        return pltpu.make_async_remote_copy(
            src_ref=total.at[lax.rem(place, 2)],
            dst_ref=maps.at[place],
            send_sem=msend_sem.at[away],
            recv_sem=mrecv_sem.at[away],
            device_id={"tm": home + lax.rem(place + away, group)},
            device_id_type=MESH,
        )

    for away in range(1, group):
        shared(away).start()
    kept = pltpu.make_async_copy(total.at[lax.rem(place, 2)], maps.at[place], own_sem.at[1])
    kept.start()
    for chunk in range(count - 1):
        heads[chunk] = spans[chunk].T

    for load in loads[2:]:
        load.wait()
    eye = diagonal(states)
    channels = lax.broadcasted_iota(jnp.int32, (states, pixels), 0)
    for k in range(n):
        projector[k] = jnp.where(
            modes[k : k + 1] == channels, weights[k : k + 1].astype(F32), 0.0
        ).astype(BF16)

    own.wait()

    @pl.loop(1, n)
    def _(away):
        piece(away).wait()

    measured = jnp.zeros((span, states), F32)
    for k in range(n):
        measured += lax.dot_general(
            regrouped[k], projector[k], (((1,), (1,)), ((), ())), preferred_element_type=F32
        )
    local[...] = lax.dot_general(
        measured.astype(BF16), gain[...], (((1,), (1,)), ((), ())), preferred_element_type=F32
    )
    held = [to_column(eye, local[c * STEPS : c * STEPS + 1]) for c in range(count)]
    for step in range(1, STEPS):
        for c in range(count):
            t = c * STEPS + step
            push = local[t : t + 1]
            if step % 2:
                held[c] = column_step(flipped[levels[t]], held[c], push)
                local[t : t + 1] = held[c]
            else:
                held[c] = row_step(eye, table[levels[t]], held[c], push)
                local[t : t + 1] = to_row(eye, held[c])
    carried = local[STEPS - 1 : STEPS]
    chunk_ends[0:1] = carried
    for c in range(1, count):
        push = local[c * STEPS + STEPS - 1 : c * STEPS + STEPS]
        if c % 2:
            carried = row_step(eye, ends[c], carried, push)
            chunk_ends[c : c + 1] = to_row(eye, carried)
        else:
            carried = column_step(ends[c], carried, push)
            chunk_ends[c : c + 1] = carried

    final = jnp.broadcast_to(chunk_ends[count - 1 : count], shift.shape)
    shift[...] = final
    shifts[place] = final

    def offsets(away):
        return pltpu.make_async_remote_copy(
            src_ref=shift,
            dst_ref=shifts.at[place],
            send_sem=csend_sem.at[away],
            recv_sem=crecv_sem.at[away],
            device_id={"tm": home + lax.rem(place + away, group)},
            device_id_type=MESH,
        )

    for away in range(1, group):
        offsets(away).start()
    kept.wait()
    for away in range(1, group):
        shared(away).wait()
    chain = maps[0].T
    for k in range(1, group):
        chain = product(maps[k] if k % 2 else maps[k].T, chain)
    whole[...] = chain
    for away in range(1, group):
        offsets(away).wait()

    moved = shifts[0, 0:1]
    for k in range(1, group):
        push = shifts[k, 0:1]
        moved = row_step(eye, maps[k], moved, push) if k % 2 else column_step(maps[k], moved, push)
    offset = moved if group % 2 else to_row(eye, moved)

    hop = pltpu.make_async_remote_copy(
        src_ref=leaving,
        dst_ref=arrived,
        send_sem=hop_send.at[0],
        recv_sem=hop_recv.at[0],
        device_id={"tm": lax.rem(me + group, n)},
        device_id_type=MESH,
    )

    @pl.when(has_last)
    def _():
        hop.wait_recv()

    @pl.when(jnp.logical_not(has_last))
    def _():
        arrived[...] = jnp.broadcast_to(start[...], arrived.shape)

    entry = arrived[0:1]

    @pl.when(has_next)
    def _():
        leaving[...] = jnp.broadcast_to(
            to_row(eye, row_step(eye, whole[...], entry, offset)), leaving.shape
        )
        hop.start()

    inside = entry
    column = to_column(eye, entry)
    for k in range(group - 1):
        push = shifts[k, 0:1]
        if k % 2:
            column = row_step(eye, maps[k], row, push)
            after = to_row(eye, column)
        else:
            row = column_step(maps[k], column, push)
            after = row
        inside = jnp.where(place == k + 1, after, inside)

    for c in range(count):
        if c:
            column = row_step(eye, heads[c - 1], inside, chunk_ends[c - 1 : c])
        else:
            column = to_column(eye, inside)
        for step in range(STEPS):
            t = c * STEPS + step
            out[t : t + 1] = column_step(prefix[t], column, local[t : t + 1])

    @pl.when(has_next)
    def _():
        hop.wait_send()


VMEM = pl.BlockSpec(memory_space=pltpu.VMEM)
SMEM = pl.BlockSpec(memory_space=pltpu.SMEM)
ANY = pl.BlockSpec(memory_space=pl.ANY)
LIMIT = 48 * 1024 * 1024


def shards(n, frames, levels, initial_state, transitions, gain, pixel_mode, pixel_weight):
    group = 4
    while n % group:
        group //= 2
    span = levels.shape[0]
    depth, states = transitions.shape[0], transitions.shape[1]
    pixels = frames.shape[0]
    count = span // STEPS
    square = (states, states)
    dma = pltpu.SemaphoreType.DMA
    return pl.pallas_call(
        functools.partial(fused_kernel, n, group),
        out_shape=jax.ShapeDtypeStruct((span, states), F32),
        in_specs=[SMEM] + [ANY] * 6,
        out_specs=VMEM,
        scratch_shapes=[
            pltpu.VMEM((pixels, n * span), BF16),
            pltpu.VMEM((n * span, pixels), BF16),
            pltpu.VMEM((n, span, pixels), BF16),
            pltpu.VMEM((depth, *square), F32),
            pltpu.VMEM((depth, *square), F32),
            pltpu.VMEM((depth, 2 * states, 2 * states), BF16),
            pltpu.VMEM((span, *square), F32),
            pltpu.VMEM((count, *square), F32),
            pltpu.VMEM((count, *square), F32),
            pltpu.VMEM((2, *square), F32),
            pltpu.VMEM((group, *square), F32),
            pltpu.VMEM(square, F32),
            pltpu.VMEM(square, BF16),
            pltpu.VMEM((n, pixels), jnp.int32),
            pltpu.VMEM((n, pixels), BF16),
            pltpu.VMEM((1, states), F32),
            pltpu.VMEM((n, states, pixels), BF16),
            pltpu.VMEM((span, states), F32),
            pltpu.VMEM((count, states), F32),
            pltpu.VMEM((8, states), F32),
            pltpu.VMEM((group, 8, states), F32),
            pltpu.VMEM((8, states), F32),
            pltpu.VMEM((8, states), F32),
            dma((6,)),
            dma((2,)),
            dma((n,)),
            dma((n,)),
            dma((group,)),
            dma((group,)),
            dma((group,)),
            dma((group,)),
            dma((1,)),
            dma((1,)),
        ],
        compiler_params=pltpu.CompilerParams(
            collective_id=0, has_side_effects=True, vmem_limit_bytes=LIMIT
        ),
        name="filter",
    )(
        levels,
        frames,
        transitions,
        gain,
        pixel_mode.reshape(n, pixels),
        pixel_weight.reshape(n, pixels),
        initial_state.reshape(1, states),
    )


def solution(mesh):
    in_specs = (P("tm", "parts"), P(("parts", "tm")), P("parts"), P(), P(), P(), P())
    out_specs = P(("parts", "tm"), None)
    return jax.shard_map(
        functools.partial(shards, mesh.shape["tm"]),
        mesh=mesh,
        in_specs=in_specs,
        out_specs=out_specs,
        check_vma=False,
    )
```

time: 46.3 us -> 29 us (0.63)
  local copies, waits for them, and re-layouts: 14.3 us -> 4.93 us
  Pallas kernels: 31.4 us -> 23.7 us
    unnamed x27 -> x15, local copies, waits for them, and re-layouts: 13.7 us -> 4.93 us
    pallas_call x5 -> x1, Pallas kernels: 31.4 us -> 23.7 us  [shards(): pl.pallas_call(functools.partial(fused_kernel, n, group), out_shape=jax.S...]
    broadcast_in_dim x2 -> x0, local copies, waits for them, and re-layouts: 0.6 us -> none  [shards(): shift = jnp.broadcast_to(chunk_ends[count - 1:], (8, states))]
where the time goes in v1:
time: 29 us; the launch traced here: 28.6 us
  Pallas kernels  23.7 us (82%)
  local copies, waits for them, and re-layouts  4.93 us (17%)
    pallas_call x1, Pallas kernels, shards(): pl.pallas_call(functools.partial(fused_kernel, n, group), out_shape=jax.S...  23.7 us
    unnamed x15, local copies, waits for them, and re-layouts  4.93 us

profile of v1, /device:TPU:24, one launch (start us, length us, event | category | flops | bytes accessed | tf_op | source)
XLA Modules:
  0.0 28.6 jit_solution(384248538109633976)
XLA Ops:
  0.0 0.0 copy-start.4
  0.0 0.0 copy-start.5
  0.0 0.0 copy-start.6
  0.0 0.7 %copy-done.4 = bf16[2048]{0:T(1024)(128)(2,1)S(1)} copy-done((bf16[2048]{0:T(1024)(128)(2,1)S(1)}, bf16[2048]{0:T(1024)(128)(2,1)}, u32[]{:S(2)}) %copy-start.4) | copy-done | bytes 4120
  0.7 0.0 copy-done.5
  0.7 0.0 copy-done.6
  0.7 0.0 copy-start
  0.7 1.2 %copy-done = f32[16,128,128]{2,1,0:T(8,128)S(1)} copy-done((f32[16,128,128]{2,1,0:T(8,128)S(1)}, f32[16,128,128]{2,1,0:T(8,128)}, u32[]{:S(2)}) %copy-start) | copy-done | bytes 1048600
  1.9 0.0 copy-start.1
  1.9 0.9 %copy-done.1 = bf16[128,1024]{1,0:T(8,128)(2,1)S(1)} copy-done((bf16[128,1024]{1,0:T(8,128)(2,1)S(1)}, bf16[128,1024]{1,0:T(8,128)(2,1)}, u32[]{:S(2)}) %copy-start.1) | copy-done | bytes 262168
  2.9 0.0 copy-start.2
  2.9 0.8 %copy-done.2 = bf16[128,128]{1,0:T(8,128)(2,1)S(1)} copy-done((bf16[128,128]{1,0:T(8,128)(2,1)S(1)}, bf16[128,128]{1,0:T(8,128)(2,1)}, u32[]{:S(2)}) %copy-start.2) | copy-done | bytes 32792
  3.6 0.0 copy-start.3
  3.6 0.7 %copy-done.3 = s32[2048]{0:T(1024)S(1)} copy-done((s32[2048]{0:T(1024)S(1)}, s32[2048]{0:T(1024)}, u32[]{:S(2)}) %copy-start.3) | copy-done | bytes 8216
  4.3 23.7 %filter.1 = f32[64,128]{1,0:T(8,128)S(1)} custom-call(s32[64]{0:T(128)S(1)} %copy-done.5, bf16[128,1024]{1,0:T(8,128)(2,1)S(1)} %copy-done.1, f32[16,128,128]{2,1,0:T(8,128)S(1)} %copy-done, bf16[128,128]{1,0:T(8,128)(2,1)S(1)} %copy-done.2, s32[16,128]{1,0:T(8,128)S(1)} %bitcast.3, bf16[16,128]{1,0:T(8,128)(2,1)S(1)} %bitcast.4, f32[1,128]{1,0:T(1,128)S(1)} %bitcast.5), custom_call_target="tpu_custom_call" | custom-call | tf_op jit(solution)/shard_map/filter/pallas_call | solution.py:305
  28.0 0.6 %copy.9 = f32[64,128]{1,0:T(8,128)} copy(f32[64,128]{1,0:T(8,128)S(1)} %filter.1) | data formatting | bytes 65536
Async XLA Ops:
  0.0 0.7 %copy-start.4 = (bf16[2048]{0:T(1024)(128)(2,1)S(1)}, bf16[2048]{0:T(1024)(128)(2,1)}, u32[]{:S(2)}) copy-start(bf16[2048]{0:T(1024)(128)(2,1)} %param.13) | copy-start | bytes 12292
  0.0 0.7 %copy-start.5 = (s32[64]{0:T(128)S(1)}, s32[64]{0:T(128)}, u32[]{:S(2)}) copy-start(s32[64]{0:T(128)} %levels.1) | copy-start | bytes 772
  0.0 0.7 %copy-start.6 = (f32[128]{0:T(128)S(1)}, f32[128]{0:T(128)}, u32[]{:S(2)}) copy-start(f32[128]{0:T(128)} %param.9) | copy-start | bytes 1540
  0.7 1.2 %copy-start = (f32[16,128,128]{2,1,0:T(8,128)S(1)}, f32[16,128,128]{2,1,0:T(8,128)}, u32[]{:S(2)}) copy-start(f32[16,128,128]{2,1,0:T(8,128)} %table_in.1) | copy-start | bytes 3145732
  1.9 0.9 %copy-start.1 = (bf16[128,1024]{1,0:T(8,128)(2,1)S(1)}, bf16[128,1024]{1,0:T(8,128)(2,1)}, u32[]{:S(2)}) copy-start(bf16[128,1024]{1,0:T(8,128)(2,1)} %frames_in.1) | copy-start | bytes 786436
  2.9 0.8 %copy-start.2 = (bf16[128,128]{1,0:T(8,128)(2,1)S(1)}, bf16[128,128]{1,0:T(8,128)(2,1)}, u32[]{:S(2)}) copy-start(bf16[128,128]{1,0:T(8,128)(2,1)} %gain_in.1) | copy-start | bytes 98308
  3.6 0.7 %copy-start.3 = (s32[2048]{0:T(1024)S(1)}, s32[2048]{0:T(1024)}, u32[]{:S(2)}) copy-start(s32[2048]{0:T(1024)} %param.12) | copy-start | bytes 24580

commit v2 on v1

--- a/solution.py
+++ b/solution.py
@@ -63,14 +63,13 @@
     levels, frames_in, table_in, gain_in, modes_in, weights_in, start_in,
     out,
     raw, turned, regrouped, table, flipped, pairs, prefix, heads, ends, total, maps, whole,
-    gain, modes, weights, start, projector, local, chunk_ends, shift, shifts, arrived, leaving,
-    load_sem, own_sem, send_sem, recv_sem, msend_sem, mrecv_sem, csend_sem, crecv_sem, hop_send, hop_recv,
+    gain, modes, weights, start, projector, local, chunk_ends, shift, shifts, block_maps, block_shifts, message, entering,
+    load_sem, own_sem, send_sem, recv_sem, msend_sem, mrecv_sem, csend_sem, crecv_sem, wsend_sem, wrecv_sem, hsend_sem, hrecv_sem,
 ):
     me = lax.axis_index("tm")
     place = lax.rem(me, group)
     home = me - place
-    has_next = me + group < n
-    has_last = me >= group
+    block, blocks = me // group, n // group
     span = out.shape[0]
     states = gain.shape[0]
     pixels = raw.shape[0]
@@ -90,8 +89,8 @@
         pl.semaphore_signal(barrier, inc=1, device_id={"tm": lax.rem(me + away, n)}, device_id_type=MESH)
 
     loads[0].wait()
-    for block in range(0, n * span, 128):
-        turned[block : block + 128] = raw[:, block : block + 128].T
+    for at in range(0, n * span, 128):
+        turned[at : at + 128] = raw[:, at : at + 128].T
     pl.semaphore_wait(barrier, n - 1)
 
     def piece(away):
@@ -166,6 +165,31 @@
             modes[k : k + 1] == channels, weights[k : k + 1].astype(F32), 0.0
         ).astype(BF16)
 
+    kept.wait()
+    for away in range(1, group):
+        shared(away).wait()
+    chain = maps[0].T
+    for k in range(1, group):
+        chain = product(maps[k] if k % 2 else maps[k].T, chain)
+    whole[...] = chain
+
+    def forward(hops):
+        return pltpu.make_async_remote_copy(
+            src_ref=whole,
+            dst_ref=block_maps.at[block],
+            send_sem=wsend_sem.at[hops],
+            recv_sem=wrecv_sem.at[hops],
+            device_id={"tm": lax.rem(me + hops * group, n)},
+            device_id_type=MESH,
+        )
+
+    for hops in range(1, blocks):
+
+        @pl.when(jnp.logical_and(block > 0, block + hops < blocks))
+        def _():
+            forward(hops).start()
+
+    seeded = jnp.where(block == 0, to_row(eye, row_step(eye, chain, start[...], 0.0)), 0.0)
     own.wait()
 
     @pl.loop(1, n)
@@ -218,13 +242,6 @@
 
     for away in range(1, group):
         offsets(away).start()
-    kept.wait()
-    for away in range(1, group):
-        shared(away).wait()
-    chain = maps[0].T
-    for k in range(1, group):
-        chain = product(maps[k] if k % 2 else maps[k].T, chain)
-    whole[...] = chain
     for away in range(1, group):
         offsets(away).wait()
 
@@ -234,32 +251,49 @@
         moved = row_step(eye, maps[k], moved, push) if k % 2 else column_step(maps[k], moved, push)
     offset = moved if group % 2 else to_row(eye, moved)
 
-    hop = pltpu.make_async_remote_copy(
-        src_ref=leaving,
-        dst_ref=arrived,
-        send_sem=hop_send.at[0],
-        recv_sem=hop_recv.at[0],
-        device_id={"tm": lax.rem(me + group, n)},
-        device_id_type=MESH,
-    )
-
-    @pl.when(has_last)
+    message[...] = jnp.broadcast_to(offset + seeded, message.shape)
+
+    def ahead(hops):
+        return pltpu.make_async_remote_copy(
+            src_ref=message,
+            dst_ref=block_shifts.at[block],
+            send_sem=hsend_sem.at[hops],
+            recv_sem=hrecv_sem.at[hops],
+            device_id={"tm": lax.rem(me + hops * group, n)},
+            device_id_type=MESH,
+        )
+
+    for hops in range(1, blocks):
+
+        @pl.when(block + hops < blocks)
+        def _():
+            ahead(hops).start()
+
+    for hops in range(1, blocks):
+
+        @pl.when(block > hops)
+        def _():
+            forward(hops).wait_recv()
+
+        @pl.when(block >= hops)
+        def _():
+            ahead(hops).wait_recv()
+
+    entering[...] = start[...]
+
+    @pl.when(block > 0)
     def _():
-        hop.wait_recv()
-
-    @pl.when(jnp.logical_not(has_last))
-    def _():
-        arrived[...] = jnp.broadcast_to(start[...], arrived.shape)
-
-    entry = arrived[0:1]
-
-    @pl.when(has_next)
-    def _():
-        leaving[...] = jnp.broadcast_to(
-            to_row(eye, row_step(eye, whole[...], entry, offset)), leaving.shape
-        )
-        hop.start()
-
+        entering[...] = block_shifts[0, 0:1]
+
+    for k in range(1, blocks - 1):
+
+        @pl.when(block > k)
+        def _():
+            entering[...] = to_row(
+                eye, row_step(eye, block_maps[k], entering[...], block_shifts[k, 0:1])
+            )
+
+    entry = entering[...]
     inside = entry
     column = to_column(eye, entry)
     for k in range(group - 1):
@@ -281,15 +315,21 @@
             t = c * STEPS + step
             out[t : t + 1] = column_step(prefix[t], column, local[t : t + 1])
 
-    @pl.when(has_next)
-    def _():
-        hop.wait_send()
+    for hops in range(1, blocks):
+
+        @pl.when(jnp.logical_and(block > 0, block + hops < blocks))
+        def _():
+            forward(hops).wait_send()
+
+        @pl.when(block + hops < blocks)
+        def _():
+            ahead(hops).wait_send()
 
 
 VMEM = pl.BlockSpec(memory_space=pltpu.VMEM)
 SMEM = pl.BlockSpec(memory_space=pltpu.SMEM)
-ANY = pl.BlockSpec(memory_space=pl.ANY)
-LIMIT = 48 * 1024 * 1024
+HBM = pl.BlockSpec(memory_space=pltpu.HBM)
+LIMIT = 63 * 1024 * 1024
 
 
 def shards(n, frames, levels, initial_state, transitions, gain, pixel_mode, pixel_weight):
@@ -305,7 +345,7 @@
     return pl.pallas_call(
         functools.partial(fused_kernel, n, group),
         out_shape=jax.ShapeDtypeStruct((span, states), F32),
-        in_specs=[SMEM] + [ANY] * 6,
+        in_specs=[SMEM] + [HBM] * 6,
         out_specs=VMEM,
         scratch_shapes=[
             pltpu.VMEM((pixels, n * span), BF16),
@@ -329,8 +369,10 @@
             pltpu.VMEM((count, states), F32),
             pltpu.VMEM((8, states), F32),
             pltpu.VMEM((group, 8, states), F32),
+            pltpu.VMEM((n // group, *square), F32),
+            pltpu.VMEM((n // group, 8, states), F32),
             pltpu.VMEM((8, states), F32),
-            pltpu.VMEM((8, states), F32),
+            pltpu.VMEM((1, states), F32),
             dma((6,)),
             dma((2,)),
             dma((n,)),
@@ -339,8 +381,10 @@
             dma((group,)),
             dma((group,)),
             dma((group,)),
-            dma((1,)),
-            dma((1,)),
+            dma((n // group,)),
+            dma((n // group,)),
+            dma((n // group,)),
+            dma((n // group,)),
         ],
         compiler_params=pltpu.CompilerParams(
             collective_id=0, has_side_effects=True, vmem_limit_bytes=LIMIT

time: 29 us -> 23.9 us (0.82)
  local copies, waits for them, and re-layouts: 4.93 us -> 1.38 us
  Pallas kernels: 23.7 us -> 22.3 us
    unnamed x15 -> x1, local copies, waits for them, and re-layouts: 4.93 us -> 1.38 us
    pallas_call x1, Pallas kernels: 23.7 us -> 22.3 us  [shards(): pl.pallas_call(functools.partial(fused_kernel, n, group), out_shape=jax.S...]
where the time goes in v2:
time: 23.9 us; the launch traced here: 23.6 us
  Pallas kernels  22.3 us (93%)
  local copies, waits for them, and re-layouts  1.38 us (6%)
    pallas_call x1, Pallas kernels, shards(): pl.pallas_call(functools.partial(fused_kernel, n, group), out_shape=jax.S...  22.3 us
    unnamed x1, local copies, waits for them, and re-layouts  1.38 us

profile of v2, /device:TPU:24, one launch (start us, length us, event | category | flops | bytes accessed | tf_op | source)
XLA Modules:
  0.0 23.6 jit_solution(2838189694092556920)
XLA Ops:
  0.0 22.3 %filter.1 = f32[64,128]{1,0:T(8,128)} custom-call(s32[64]{0:T(128)} %levels.1, bf16[128,1024]{1,0:T(8,128)(2,1)} %frames_in.1, f32[16,128,128]{2,1,0:T(8,128)} %table_in.1, bf16[128,128]{1,0:T(8,128)(2,1)} %gain_in.1, s32[16,128]{1,0:T(8,128)} %bitcast.3, bf16[16,128]{1,0:T(8,128)(2,1)} %bitcast.4, f32[1,128]{1,0:T(1,128)} %bitcast.5), custom_call_target="tpu_custom_call" | custom-call | tf_op jit(solution)/shard_map/filter/pallas_call | solution.py:345
  22.3 1.4 %copy.9 = f32[64,128]{1,0:T(8,128)} copy(f32[64,128]{1,0:T(8,128)} %filter.1) | data formatting | bytes 65536

commit v3 on v2

--- a/solution.py
+++ b/solution.py
@@ -91,6 +91,11 @@
     loads[0].wait()
     for at in range(0, n * span, 128):
         turned[at : at + 128] = raw[:, at : at + 128].T
+    loads[1].wait()
+    for level in range(table.shape[0]):
+        other = table[level].T
+        flipped[level] = other
+        pairs[level] = right_pair(other)
     pl.semaphore_wait(barrier, n - 1)
 
     def piece(away):
@@ -104,20 +109,15 @@
             device_id_type=MESH,
         )
 
-    @pl.loop(1, n)
-    def _(away):
-        piece(away).start()
+    @pl.loop(0, n - 1)
+    def _(turn):
+        piece(n // 2 + (1 - 2 * lax.rem(turn, 2)) * ((turn + 1) // 2)).start()
 
     own = pltpu.make_async_copy(
         turned.at[pl.ds(pl.multiple_of(me * span, span), span)], regrouped.at[me], own_sem.at[0]
     )
     own.start()
 
-    loads[1].wait()
-    for level in range(table.shape[0]):
-        other = table[level].T
-        flipped[level] = other
-        pairs[level] = right_pair(other)
     for chunk in range(count):
         prefix[chunk * STEPS] = flipped[levels[chunk * STEPS]]
     for step in range(1, STEPS):
@@ -165,31 +165,6 @@
             modes[k : k + 1] == channels, weights[k : k + 1].astype(F32), 0.0
         ).astype(BF16)
 
-    kept.wait()
-    for away in range(1, group):
-        shared(away).wait()
-    chain = maps[0].T
-    for k in range(1, group):
-        chain = product(maps[k] if k % 2 else maps[k].T, chain)
-    whole[...] = chain
-
-    def forward(hops):
-        return pltpu.make_async_remote_copy(
-            src_ref=whole,
-            dst_ref=block_maps.at[block],
-            send_sem=wsend_sem.at[hops],
-            recv_sem=wrecv_sem.at[hops],
-            device_id={"tm": lax.rem(me + hops * group, n)},
-            device_id_type=MESH,
-        )
-
-    for hops in range(1, blocks):
-
-        @pl.when(jnp.logical_and(block > 0, block + hops < blocks))
-        def _():
-            forward(hops).start()
-
-    seeded = jnp.where(block == 0, to_row(eye, row_step(eye, chain, start[...], 0.0)), 0.0)
     own.wait()
 
     @pl.loop(1, n)
@@ -242,6 +217,31 @@
 
     for away in range(1, group):
         offsets(away).start()
+    kept.wait()
+    for away in range(1, group):
+        shared(away).wait()
+    chain = maps[0].T
+    for k in range(1, group):
+        chain = product(maps[k] if k % 2 else maps[k].T, chain)
+    whole[...] = chain
+
+    def forward(hops):
+        return pltpu.make_async_remote_copy(
+            src_ref=whole,
+            dst_ref=block_maps.at[block],
+            send_sem=wsend_sem.at[hops],
+            recv_sem=wrecv_sem.at[hops],
+            device_id={"tm": lax.rem(me + hops * group, n)},
+            device_id_type=MESH,
+        )
+
+    for hops in range(1, blocks):
+
+        @pl.when(jnp.logical_and(block > 0, block + hops < blocks))
+        def _():
+            forward(hops).start()
+
+    seeded = jnp.where(block == 0, to_row(eye, row_step(eye, chain, start[...], 0.0)), 0.0)
     for away in range(1, group):
         offsets(away).wait()
 

time: 23.9 us -> 22.2 us (0.929)
  Pallas kernels: 22.3 us -> 20.6 us
    pallas_call x1, Pallas kernels: 22.3 us -> 20.6 us  [shards(): pl.pallas_call(functools.partial(fused_kernel, n, group), out_shape=jax.S...]
where the time goes in v3:
time: 22.2 us; the launch traced here: 21.9 us
  Pallas kernels  20.6 us (93%)
  local copies, waits for them, and re-layouts  1.38 us (6%)
    pallas_call x1, Pallas kernels, shards(): pl.pallas_call(functools.partial(fused_kernel, n, group), out_shape=jax.S...  20.6 us
    unnamed x1, local copies, waits for them, and re-layouts  1.38 us

profile of v3, /device:TPU:24, one launch (start us, length us, event | category | flops | bytes accessed | tf_op | source)
XLA Modules:
  0.0 21.9 jit_solution(12427472121063944815)
XLA Ops:
  0.0 20.6 %filter.1 = f32[64,128]{1,0:T(8,128)} custom-call(s32[64]{0:T(128)} %levels.1, bf16[128,1024]{1,0:T(8,128)(2,1)} %frames_in.1, f32[16,128,128]{2,1,0:T(8,128)} %table_in.1, bf16[128,128]{1,0:T(8,128)(2,1)} %gain_in.1, s32[16,128]{1,0:T(8,128)} %bitcast.3, bf16[16,128]{1,0:T(8,128)(2,1)} %bitcast.4, f32[1,128]{1,0:T(1,128)} %bitcast.5), custom_call_target="tpu_custom_call" | custom-call | tf_op jit(solution)/shard_map/filter/pallas_call | solution.py:345
  20.6 1.4 %copy.9 = f32[64,128]{1,0:T(8,128)} copy(f32[64,128]{1,0:T(8,128)} %filter.1) | data formatting | bytes 65536

commit v4 on v3

--- a/solution.py
+++ b/solution.py
@@ -127,17 +127,12 @@
                 jnp.dot(left_pair(prefix[t - 1]), pairs[levels[t]], preferred_element_type=F32)
             )
     spans = [prefix[chunk * STEPS + STEPS - 1] for chunk in range(count)]
-    for chunk in range(count):
-        ends[chunk] = spans[chunk].T if chunk % 2 else spans[chunk]
-    width = 1
-    while width < count:
-        for chunk in range(count):
-            if chunk & width:
-                base = (chunk // width) * width - 1
-                spans[chunk] = product(spans[base], spans[chunk])
-        width *= 2
-    total[0] = spans[count - 1]
-    total[1] = spans[count - 1].T
+    tree = [spans]
+    while len(tree[-1]) > 1:
+        last = tree[-1]
+        tree.append([product(last[2 * k], last[2 * k + 1]) for k in range(len(last) // 2)])
+    total[0] = tree[-1][0]
+    total[1] = tree[-1][0].T
 
     def shared(away):
         return pltpu.make_async_remote_copy(
@@ -153,8 +148,15 @@
         shared(away).start()
     kept = pltpu.make_async_copy(total.at[lax.rem(place, 2)], maps.at[place], own_sem.at[1])
     kept.start()
-    for chunk in range(count - 1):
-        heads[chunk] = spans[chunk].T
+    for chunk in range(count):
+        ends[chunk] = spans[chunk].T if chunk % 2 else spans[chunk]
+    reached = [None]
+    for upto in range(1, count):
+        rank = (upto & -upto).bit_length() - 1
+        node = tree[rank][(upto >> rank) - 1]
+        before = reached[upto - (1 << rank)]
+        reached.append(node if before is None else product(before, node))
+        heads[upto - 1] = reached[upto].T
 
     for load in loads[2:]:
         load.wait()

time: 22.2 us -> 22.2 us (level)
  no operation moved by 1% of the time
where the time goes in v4:
time: 22.2 us; the launch traced here: 21.9 us
  Pallas kernels  20.6 us (93%)
  local copies, waits for them, and re-layouts  1.38 us (6%)
    pallas_call x1, Pallas kernels, shards(): pl.pallas_call(functools.partial(fused_kernel, n, group), out_shape=jax.S...  20.6 us
    unnamed x1, local copies, waits for them, and re-layouts  1.38 us

profile of v4, /device:TPU:24, one launch (start us, length us, event | category | flops | bytes accessed | tf_op | source)
XLA Modules:
  0.0 21.9 jit_solution(471278112873084466)
XLA Ops:
  0.0 20.6 %filter.1 = f32[64,128]{1,0:T(8,128)} custom-call(s32[64]{0:T(128)} %levels.1, bf16[128,1024]{1,0:T(8,128)(2,1)} %frames_in.1, f32[16,128,128]{2,1,0:T(8,128)} %table_in.1, bf16[128,128]{1,0:T(8,128)(2,1)} %gain_in.1, s32[16,128]{1,0:T(8,128)} %bitcast.3, bf16[16,128]{1,0:T(8,128)(2,1)} %bitcast.4, f32[1,128]{1,0:T(1,128)} %bitcast.5), custom_call_target="tpu_custom_call" | custom-call | tf_op jit(solution)/shard_map/filter/pallas_call | solution.py:347
  20.6 1.4 %copy.9 = f32[64,128]{1,0:T(8,128)} copy(f32[64,128]{1,0:T(8,128)} %filter.1) | data formatting | bytes 65536
